TPU v7x, 32 devices: a whole 2x2x4 slice. The times are simulated.
32 devices in a mesh: groups: 2 (over x), blk: 8 (over z, y), split: 2 (over core).
Axes of the slice: x: 2, y: 2, z: 4, core: 2. Of those that a mesh axis runs over, the one named last changes fastest.
Arguments:
- embeddings: bfloat16 [32768, 768], P(('groups', 'blk', 'split')), parts along dimension 0, may hold values from -6 to 6
- cluster_of: int32 [32768], P(('groups', 'blk', 'split')), parts along dimension 0, may hold values from 0 to 15, as said below
- target_pos: int32 [32768], P(('groups', 'blk', 'split')), parts along dimension 0, may hold values from 0 to 16383, as said below
Outputs:
- best: float32 [32768], P(('groups', 'blk', 'split')), parts along dimension 0
There are 2 independent parts, one for each index of `groups`. A program takes and returns all parts, laid end to end along the dimension named above; each array names one. Nothing has to cross between parts.
Inputs may be any that keep to these rules, and one draw needn't show every extreme that they name: `cluster_of`: ordering the members by target_pos lists cluster 0 first, then cluster 1 and so on, each cluster's members contiguous; every cluster has 2 to 4096 members and one has exactly 4096. `target_pos`: A permutation of the rows. For every aligned block of 1024 positions, each device's 1024 data-order rows hold exactly 64 of its positions.
All inputs are finite; a program needn't handle non-finite values.
Results may differ from a plain program's by a relative error of at most 0.0025.
Values may be sent and summed in bfloat16 or wider, within the bound.
A program may use at most 64 MiB of HBM per device.

v0:
```python
import jax
import jax.numpy as jnp
from jax import lax
from jax.sharding import PartitionSpec as P

MOST = 4096
FILL = -4.0


def from_behind(block, axis, distance):
    devices = range(lax.axis_size(axis))
    route = [((i - distance) % len(devices), i) for i in devices]
    return lax.ppermute(block, axis, route)


def masked_scores(left, left_ids, right, right_ids):
    sims = lax.dot_general(
        left, right, (((1,), (1,)), ((), ())), preferred_element_type=jnp.float32
    )
    return jnp.where(left_ids[:, None] == right_ids[None, :], sims, FILL)


def body(embeddings, cluster_of, target_pos):
    count = lax.axis_size(("blk", "split"))
    rows, width = embeddings.shape
    piece = rows // count
    me = lax.axis_index(("blk", "split"))
    values = embeddings.astype(jnp.float32)
    unit = (values * lax.rsqrt(jnp.sum(values * values, axis=1, keepdims=True) + 1e-06)).astype(
        jnp.bfloat16
    )
    order = jnp.argsort(target_pos)
    packed = unit[order].reshape(count, piece, width)
    labels = jnp.stack(
        [cluster_of[order].reshape(count, piece), target_pos[order].reshape(count, piece)], axis=1
    )
    received, tags = (
        lax.all_to_all(packed, ("blk", "split"), split_axis=0, concat_axis=0, tiled=True),
        lax.all_to_all(labels, ("blk", "split"), split_axis=0, concat_axis=0, tiled=True),
    )
    unit_in = received.reshape(rows, width)
    ids_in = tags[:, 0, :].reshape(rows)
    local = tags[:, 1, :].reshape(rows) - me * rows
    place = jnp.argsort(local)
    mine = unit_in[place]
    my_ids = ids_in[place]
    reach = (MOST + rows - 2) // rows
    own = masked_scores(mine, my_ids, mine, my_ids)
    diagonal = jnp.arange(rows)[:, None] == jnp.arange(rows)[None, :]
    best = jnp.max(jnp.where(diagonal, FILL, own), axis=1)

    def both_maxima(pair, visit_unit, visit_ids):
        row_best, visit_best = pair
        scores = masked_scores(mine, my_ids, visit_unit, visit_ids)
        return (
            jnp.maximum(row_best, jnp.max(scores, axis=1)),
            jnp.maximum(visit_best, jnp.max(scores, axis=0)),
        )

    def turn(step, carry):
        row_best, visit_unit, visit_ids, visit_best = carry
        visit_unit, visit_ids, visit_best = (
            from_behind(visit_unit, ("blk", "split"), 1),
            from_behind(visit_ids, ("blk", "split"), 1),
            from_behind(visit_best.astype(jnp.bfloat16), ("blk", "split"), 1).astype(
                visit_best.dtype
            ),
        )
        row_best, visit_best = both_maxima((row_best, visit_best), visit_unit, visit_ids)
        return (row_best, visit_unit, visit_ids, visit_best)

    start_best = jnp.full((rows,), FILL, jnp.float32)
    best, visit_unit, visit_ids, visit_best = lax.fori_loop(
        0, reach, turn, (best, mine, my_ids, start_best)
    )
    returned_home = from_behind(visit_best, ("blk", "split"), -reach)
    best = jnp.maximum(best, returned_home)
    back = best[local].reshape(count, piece)
    returned = lax.all_to_all(
        back, ("blk", "split"), split_axis=0, concat_axis=0, tiled=True
    ).reshape(rows)
    return jnp.zeros((rows,), jnp.float32).at[order].set(returned)


def solution(mesh):
    return jax.shard_map(
        body,
        mesh=mesh,
        in_specs=(
            P(("groups", "blk", "split"), None),
            P(("groups", "blk", "split")),
            P(("groups", "blk", "split")),
        ),
        out_specs=P(("groups", "blk", "split")),
        check_vma=False,
    )
```

profile of v0, /device:TPU:0, one launch (start us, length us, event | category | flops | bytes accessed | tf_op | source)
XLA Modules:
  0.0 204.1 jit_solution(9965459332306292172)
XLA Ops:
  0.0 5.1 %sort.31 = (s32[1024]{0:T(1024)}, s32[1024]{0:T(1024)S(1)}) sort(s32[1024]{0:T(1024)} %param.7, s32[1024]{0:T(1024)S(1)} %iota.15), dimensions={0}, to_apply=%region_0.0 | sort | flops 10240 | bytes 16384 | tf_op jit(solution)/shard_map/jit(argsort)/sort | solution.py:32
  5.1 4.5 %gather_fusion.1 = s32[1024]{0:T(1024)S(1)} fusion(s32[1024]{0:T(1024)S(1)} %copy-done.1, s32[1024]{0:T(1024)S(1)} %get-tuple-element.92), kind=kCustom, calls=%fused_computation.1 | custom fusion | bytes 12288 | tf_op jit(solution)/shard_map/gather | solution.py:35
  9.7 0.1 stack_reshape.7
  9.8 4.5 %gather_fusion = s32[1024]{0:T(1024)S(1)} fusion(s32[1024]{0:T(1024)S(1)} %copy-done, s32[1024]{0:T(1024)S(1)} %get-tuple-element.92), kind=kCustom, calls=%fused_computation | custom fusion | bytes 12288 | tf_op jit(solution)/shard_map/gather | solution.py:35
  14.3 0.1 stack_reshape.6
  14.4 0.7 reshape.140
  15.1 7.4 %all-to-all-start = ((s32[16,1,128]{2,1,0:T(1,128)}), s32[16,1,128]{2,1,0:T(1,128)S(1)}, u32[]{:S(2)}, u32[]{:S(2)}) async-start(s32[16,1,128]{2,1,0:T(1,128)} %reshape.140), calls=%async_computation | async-start | bytes 16384 | tf_op jit(solution)/shard_map/all_to_all | solution.py:39
  22.5 0.4 fusion.2
  22.9 0.3 fusion.3
  23.2 5.2 %gather_fusion.3 = bf16[1024,768]{1,0:T(8,128)(2,1)} fusion(bf16[1024,768]{1,0:T(8,128)(2,1)S(1)} %fusion.3, s32[1024]{0:T(1024)S(1)} %get-tuple-element.92), kind=kCustom, calls=%fused_computation.3 | custom fusion | bytes 3149824 | tf_op jit(solution)/shard_map/gather | solution.py:33
  28.4 0.5 all-to-all-done
  28.9 5.5 %all-to-all-start.1 = ((bf16[16,64,768]{2,1,0:T(8,128)(2,1)}), bf16[16,64,768]{2,1,0:T(8,128)(2,1)S(1)}, u32[]{:S(2)}, u32[]{:S(2)}) async-start(bf16[16,64,768]{2,1,0:T(8,128)(2,1)} %bitcast), calls=%async_computation.1 | async-start | bytes 3145728 | tf_op jit(solution)/shard_map/all_to_all | solution.py:38
  34.5 0.5 broadcast.95
  35.0 0.7 reduce.15
  35.7 0.1 reshape.141
  35.8 0.5 broadcast.93
  36.3 0.7 fusion.7
  37.0 0.1 sub.21
  37.0 0.1 sub.22
  37.1 0.1 reshape_squeeze.4
  37.2 4.4 %sort.32 = (s32[1024]{0:T(1024)}, s32[1024]{0:T(1024)S(1)}) sort(s32[1024]{0:T(1024)S(1)} %sub.21, s32[1024]{0:T(1024)S(1)} %iota.16), dimensions={0}, to_apply=%region_1.0 | sort | flops 10240 | bytes 16384 | tf_op jit(solution)/shard_map/jit(argsort)/sort | solution.py:44
  41.6 4.5 %gather_fusion.2 = s32[1024]{0:T(1024)S(1)} fusion(s32[1024]{0:T(1024)S(1)} %reshape_squeeze.4, s32[1024]{0:T(1024)S(1)} %fusion.4), kind=kCustom, calls=%fused_computation.2 | custom fusion | bytes 12288 | tf_op jit(solution)/shard_map/gather | solution.py:46
  46.1 20.2 %all-to-all-done.1 = bf16[16,64,768]{2,1,0:T(8,128)(2,1)S(1)} async-done(((bf16[16,64,768]{2,1,0:T(8,128)(2,1)}), bf16[16,64,768]{2,1,0:T(8,128)(2,1)S(1)}, u32[]{:S(2)}, u32[]{:S(2)}) %all-to-all-start.1) | async-done | bytes 1572896 | tf_op jit(solution)/shard_map/all_to_all | solution.py:38
  66.3 4.0 %gather_fusion.4 = bf16[1024,768]{1,0:T(8,128)(2,1)S(1)} fusion(bf16[1024,768]{1,0:T(8,128)(2,1)S(1)} %bitcast.13, s32[1024]{0:T(1024)S(1)} %fusion.4), kind=kCustom, calls=%fused_computation.4 | custom fusion | bytes 3149824 | tf_op jit(solution)/shard_map/gather | solution.py:45
  70.3 1.8 select_reduce_fusion
  72.1 1.2 copy.6
  73.3 107.0 %while.17 = (s32[]{:T(128)}, f32[1024]{0:T(1024)S(1)}, bf16[1024,768]{1,0:T(8,128)(2,1)}, s32[1024]{0:T(1024)S(1)}, f32[1024]{0:T(1024)S(1)}, /*index=5*/s32[102...) while((s32[]{:T(128)}, f32[1024]{0:T(1024)S(1)}, bf16[1024,768]{1,0:T(8,128)(2,1)}, ...), condition=%wide.region_7.8_spmd.clone, body=%wide.region_4.0_spmd.clone.sunk | while | flops 1614809088 | bytes 12660959 | solution.py:73
  73.3 1.0 collective-permute-start.1
  74.3 1.8 collective-permute-start
  76.1 1.0 collective-permute-start.2
  77.1 22.3 %collective-permute-done = s32[1024]{0:T(1024)S(1)} collective-permute-done((s32[1024]{0:T(1024)S(1)}, s32[1024]{0:T(1024)S(1)}, u32[]{:S(2)}, u32[]{:S(2)}) %collective-permute-start) | collective-permute-done | bytes 4128 | tf_op jit(solution)/shard_map/while/body/eval_jaxpr/ppermute | solution.py:13
  99.4 1.9 fusion.17
  101.3 1.2 copy.16
  102.5 0.0 collective-permute-done.2
  102.5 0.0 collective-permute-start.1
  102.5 0.1 collective-permute-start
  102.6 0.1 collective-permute-start.2
  102.7 22.6 %collective-permute-done = s32[1024]{0:T(1024)S(1)} collective-permute-done((s32[1024]{0:T(1024)S(1)}, s32[1024]{0:T(1024)S(1)}, u32[]{:S(2)}, u32[]{:S(2)}) %collective-permute-start) | collective-permute-done | bytes 4128 | tf_op jit(solution)/shard_map/while/body/eval_jaxpr/ppermute | solution.py:13
  125.3 0.0 collective-permute-done.1
  125.3 1.9 fusion.17
  127.2 1.2 copy.16
  128.4 0.0 collective-permute-done.2
  128.4 0.1 collective-permute-start
  128.5 0.1 collective-permute-start.2
  128.6 22.6 %collective-permute-done = s32[1024]{0:T(1024)S(1)} collective-permute-done((s32[1024]{0:T(1024)S(1)}, s32[1024]{0:T(1024)S(1)}, u32[]{:S(2)}, u32[]{:S(2)}) %collective-permute-start) | collective-permute-done | bytes 4128 | tf_op jit(solution)/shard_map/while/body/eval_jaxpr/ppermute | solution.py:13
  151.2 0.0 collective-permute-done.1
  151.2 1.9 fusion.17
  153.1 1.2 copy.16
  154.3 0.0 collective-permute-done.2
  154.3 0.1 collective-permute-start
  154.4 0.1 collective-permute-start.2
  154.5 22.7 %collective-permute-done = s32[1024]{0:T(1024)S(1)} collective-permute-done((s32[1024]{0:T(1024)S(1)}, s32[1024]{0:T(1024)S(1)}, u32[]{:S(2)}, u32[]{:S(2)}) %collective-permute-start) | collective-permute-done | bytes 4128 | tf_op jit(solution)/shard_map/while/body/eval_jaxpr/ppermute | solution.py:13
  177.2 1.9 fusion.17
  179.2 1.2 copy.16
  180.3 0.0 collective-permute-done.2
  180.3 0.0 collective-permute-start.3
  180.3 3.6 %collective-permute-done.3 = f32[1024]{0:T(1024)S(1)} collective-permute-done((f32[1024]{0:T(1024)S(1)}, f32[1024]{0:T(1024)S(1)}, u32[]{:S(2)}, u32[]{:S(2)}) %collective-permute-start.3) | collective-permute-done | bytes 4128 | tf_op jit(solution)/shard_map/ppermute | solution.py:13
  183.9 4.5 %gather_fusion.5 = f32[1024]{0:T(1024)S(1)} fusion(f32[1024]{0:T(1024)S(1)} %max.9, s32[1024]{0:T(1024)S(1)} %broadcast_clamp_fusion), kind=kCustom, calls=%fused_computation.5 | custom fusion | bytes 12288 | tf_op jit(solution)/shard_map/gather | solution.py:78
  188.5 0.1 all_to_all.14
  188.5 9.4 %all_to_all.19 = f32[16,1,64]{2,1,0:T(1,128)S(1)} all-to-all(f32[16,1,64]{2,1,0:T(1,128)S(1)} %all_to_all.14), channel_id=1, replica_groups=mesh['groups'=2,'blk'=8,'split'=2] {'blk','split'}, dimensions={0} | all-to-all | bytes 8192 | tf_op jit(solution)/shard_map/all_to_all | solution.py:79
  197.9 0.5 broadcast.94
  198.5 0.7 reduce.13
  199.1 0.1 reshape.102
  199.2 4.9 %scatter_custom_fusion = f32[1024]{0:T(1024)} fusion(s32[1024]{0:T(1024)S(1)} %get-tuple-element.93, f32[1024]{0:T(1024)S(1)} %reshape.102, f32[]{:T(128)} %constant.3.clone.1), kind=kCustom, calls=%fused_computation.28 | custom fusion | bytes 4100 | tf_op jit(solution)/shard_map/scatter | solution.py:82
  (37 shorter events, 0.2 us)
Async XLA Ops:
  0.0 9.8 %copy-start = (s32[1024]{0:T(1024)S(1)}, s32[1024]{0:T(1024)}, u32[]{:S(2)}) copy-start(s32[1024]{0:T(1024)} %param.6) | copy-start | bytes 12292
  0.0 5.1 %copy-start.1 = (s32[1024]{0:T(1024)S(1)}, s32[1024]{0:T(1024)}, u32[]{:S(2)}) copy-start(s32[1024]{0:T(1024)} %param.7) | copy-start | bytes 12292
  9.8 12.7 %copy-start.2 = (bf16[1024,768]{1,0:T(8,128)(2,1)S(1)}, bf16[1024,768]{1,0:T(8,128)(2,1)}, u32[]{:S(2)}) copy-start(bf16[1024,768]{1,0:T(8,128)(2,1)} %param.5) | copy-start | bytes 4718596
  15.1 13.8 %all-to-all-start = ((s32[16,1,128]{2,1,0:T(1,128)}), s32[16,1,128]{2,1,0:T(1,128)S(1)}, u32[]{:S(2)}, u32[]{:S(2)}) async-start(s32[16,1,128]{2,1,0:T(1,128)} %reshape.140), calls=%async_computation | async-start | bytes 16384 | tf_op jit(solution)/shard_map/all_to_all | solution.py:39
  28.9 37.4 %all-to-all-start.1 = ((bf16[16,64,768]{2,1,0:T(8,128)(2,1)}), bf16[16,64,768]{2,1,0:T(8,128)(2,1)S(1)}, u32[]{:S(2)}, u32[]{:S(2)}) async-start(bf16[16,64,768]{2,1,0:T(8,128)(2,1)} %bitcast), calls=%async_computation.1 | async-start | bytes 3145728 | tf_op jit(solution)/shard_map/all_to_all | solution.py:38
  73.3 26.1 %collective-permute-start.1 = (bf16[1024,768]{1,0:T(8,128)(2,1)}, bf16[1024,768]{1,0:T(8,128)(2,1)S(1)}, u32[]{:S(2)}, u32[]{:S(2)}) collective-permute-start(bf16[1024,768]{1,0:T(8,128)(2,1)} %get-tuple-element.152), channel_id=1, source_target_pairs={{15,0},{0,1},{1,2},{2,3},{3,4},{4,5},{5,6},{6,7},{7,8},{8,9},{9,10... | collective-permute-start | bytes 4718600 | tf_op jit(solution)/shard_map/while/body/eval_jaxpr/ppermute | solution.py:13
  74.3 25.1 %collective-permute-start = (s32[1024]{0:T(1024)S(1)}, s32[1024]{0:T(1024)S(1)}, u32[]{:S(2)}, u32[]{:S(2)}) collective-permute-start(s32[1024]{0:T(1024)S(1)} %get-tuple-element.153), channel_id=1, source_target_pairs={{15,0},{0,1},{1,2},{2,3},{3,4},{4,5},{5,6},{6,7},{7,8},{8,9},{9,10... | collective-permute-start | bytes 12296 | tf_op jit(solution)/shard_map/while/body/eval_jaxpr/ppermute | solution.py:13
  76.1 26.4 %collective-permute-start.2 = (bf16[1024]{0:T(1024)(128)(2,1)S(1)}, bf16[1024]{0:T(1024)(128)(2,1)S(1)}, u32[]{:S(2)}, u32[]{:S(2)}) collective-permute-start(bf16[1024]{0:T(1024)(128)(2,1)S(1)} %select_convert_fusion.2), channel_id=1, source_target_pairs={{15,0},{0,1},{1,2},{2,3},{3,4},{4,5},{5,6},{6,7},{7,8},{8,9},{9,10... | collective-permute-start | bytes 6152 | tf_op jit(solution)/shard_map/while/body/eval_jaxpr/ppermute | solution.py:13
  102.5 22.8 %collective-permute-start.1 = (bf16[1024,768]{1,0:T(8,128)(2,1)}, bf16[1024,768]{1,0:T(8,128)(2,1)S(1)}, u32[]{:S(2)}, u32[]{:S(2)}) collective-permute-start(bf16[1024,768]{1,0:T(8,128)(2,1)} %get-tuple-element.152), channel_id=1, source_target_pairs={{15,0},{0,1},{1,2},{2,3},{3,4},{4,5},{5,6},{6,7},{7,8},{8,9},{9,10... | collective-permute-start | bytes 4718600 | tf_op jit(solution)/shard_map/while/body/eval_jaxpr/ppermute | solution.py:13
  102.5 22.8 %collective-permute-start = (s32[1024]{0:T(1024)S(1)}, s32[1024]{0:T(1024)S(1)}, u32[]{:S(2)}, u32[]{:S(2)}) collective-permute-start(s32[1024]{0:T(1024)S(1)} %get-tuple-element.153), channel_id=1, source_target_pairs={{15,0},{0,1},{1,2},{2,3},{3,4},{4,5},{5,6},{6,7},{7,8},{8,9},{9,10... | collective-permute-start | bytes 12296 | tf_op jit(solution)/shard_map/while/body/eval_jaxpr/ppermute | solution.py:13
  102.6 25.8 %collective-permute-start.2 = (bf16[1024]{0:T(1024)(128)(2,1)S(1)}, bf16[1024]{0:T(1024)(128)(2,1)S(1)}, u32[]{:S(2)}, u32[]{:S(2)}) collective-permute-start(bf16[1024]{0:T(1024)(128)(2,1)S(1)} %select_convert_fusion.2), channel_id=1, source_target_pairs={{15,0},{0,1},{1,2},{2,3},{3,4},{4,5},{5,6},{6,7},{7,8},{8,9},{9,10... | collective-permute-start | bytes 6152 | tf_op jit(solution)/shard_map/while/body/eval_jaxpr/ppermute | solution.py:13
  128.4 22.8 %collective-permute-start.1 = (bf16[1024,768]{1,0:T(8,128)(2,1)}, bf16[1024,768]{1,0:T(8,128)(2,1)S(1)}, u32[]{:S(2)}, u32[]{:S(2)}) collective-permute-start(bf16[1024,768]{1,0:T(8,128)(2,1)} %get-tuple-element.152), channel_id=1, source_target_pairs={{15,0},{0,1},{1,2},{2,3},{3,4},{4,5},{5,6},{6,7},{7,8},{8,9},{9,10... | collective-permute-start | bytes 4718600 | tf_op jit(solution)/shard_map/while/body/eval_jaxpr/ppermute | solution.py:13
  128.4 22.8 %collective-permute-start = (s32[1024]{0:T(1024)S(1)}, s32[1024]{0:T(1024)S(1)}, u32[]{:S(2)}, u32[]{:S(2)}) collective-permute-start(s32[1024]{0:T(1024)S(1)} %get-tuple-element.153), channel_id=1, source_target_pairs={{15,0},{0,1},{1,2},{2,3},{3,4},{4,5},{5,6},{6,7},{7,8},{8,9},{9,10... | collective-permute-start | bytes 12296 | tf_op jit(solution)/shard_map/while/body/eval_jaxpr/ppermute | solution.py:13
  128.5 25.8 %collective-permute-start.2 = (bf16[1024]{0:T(1024)(128)(2,1)S(1)}, bf16[1024]{0:T(1024)(128)(2,1)S(1)}, u32[]{:S(2)}, u32[]{:S(2)}) collective-permute-start(bf16[1024]{0:T(1024)(128)(2,1)S(1)} %select_convert_fusion.2), channel_id=1, source_target_pairs={{15,0},{0,1},{1,2},{2,3},{3,4},{4,5},{5,6},{6,7},{7,8},{8,9},{9,10... | collective-permute-start | bytes 6152 | tf_op jit(solution)/shard_map/while/body/eval_jaxpr/ppermute | solution.py:13
  154.3 22.9 %collective-permute-start.1 = (bf16[1024,768]{1,0:T(8,128)(2,1)}, bf16[1024,768]{1,0:T(8,128)(2,1)S(1)}, u32[]{:S(2)}, u32[]{:S(2)}) collective-permute-start(bf16[1024,768]{1,0:T(8,128)(2,1)} %get-tuple-element.152), channel_id=1, source_target_pairs={{15,0},{0,1},{1,2},{2,3},{3,4},{4,5},{5,6},{6,7},{7,8},{8,9},{9,10... | collective-permute-start | bytes 4718600 | tf_op jit(solution)/shard_map/while/body/eval_jaxpr/ppermute | solution.py:13
  154.3 22.9 %collective-permute-start = (s32[1024]{0:T(1024)S(1)}, s32[1024]{0:T(1024)S(1)}, u32[]{:S(2)}, u32[]{:S(2)}) collective-permute-start(s32[1024]{0:T(1024)S(1)} %get-tuple-element.153), channel_id=1, source_target_pairs={{15,0},{0,1},{1,2},{2,3},{3,4},{4,5},{5,6},{6,7},{7,8},{8,9},{9,10... | collective-permute-start | bytes 12296 | tf_op jit(solution)/shard_map/while/body/eval_jaxpr/ppermute | solution.py:13
  154.4 25.9 %collective-permute-start.2 = (bf16[1024]{0:T(1024)(128)(2,1)S(1)}, bf16[1024]{0:T(1024)(128)(2,1)S(1)}, u32[]{:S(2)}, u32[]{:S(2)}) collective-permute-start(bf16[1024]{0:T(1024)(128)(2,1)S(1)} %select_convert_fusion.2), channel_id=1, source_target_pairs={{15,0},{0,1},{1,2},{2,3},{3,4},{4,5},{5,6},{6,7},{7,8},{8,9},{9,10... | collective-permute-start | bytes 6152 | tf_op jit(solution)/shard_map/while/body/eval_jaxpr/ppermute | solution.py:13
  180.3 3.6 %collective-permute-start.3 = (f32[1024]{0:T(1024)S(1)}, f32[1024]{0:T(1024)S(1)}, u32[]{:S(2)}, u32[]{:S(2)}) collective-permute-start(f32[1024]{0:T(1024)S(1)} %get-tuple-element.48), channel_id=1, source_target_pairs={{4,0},{5,1},{6,2},{7,3},{8,4},{9,5},{10,6},{11,7},{12,8},{13,9},{1... | collective-permute-start | bytes 12296 | tf_op jit(solution)/shard_map/ppermute | solution.py:13
where the time goes:
time: 204 us
  waiting for transfers between devices  115 us (56%)
  local copies, waits for them, and re-layouts  40.8 us (20%)
  starting transfers between devices  17.1 us (8%)
  other arithmetic  12.3 us (6%)
  matrix products  9.56 us (5%)
  blocking collectives  9.41 us (5%)
    ppermute x13, waiting for transfers between devices, from_behind(): return lax.ppermute(block, axis, route)  93.9 us
    all_to_all x1, waiting for transfers between devices, body(): lax.all_to_all(packed, ('blk', 'split'), split_axis=0, concat_axis=0, til...  20.2 us
    dot_general x5, matrix products, masked_scores(): lax.dot_general(left, right, (((1,), (1,)), ((), ())), preferred_element_...  9.56 us
    all_to_all x1, blocking collectives, body(): lax.all_to_all(back, ('blk', 'split'), split_axis=0, concat_axis=0, tiled...  9.41 us
    all_to_all x1, starting transfers between devices, body(): lax.all_to_all(labels, ('blk', 'split'), split_axis=0, concat_axis=0, til...  7.41 us
    all_to_all x1, starting transfers between devices, body(): lax.all_to_all(packed, ('blk', 'split'), split_axis=0, concat_axis=0, til...  5.53 us
    gather x1, local copies, waits for them, and re-layouts, body(): packed = unit[order].reshape(count, piece, width)  5.21 us
    sort x1, other arithmetic, body(): order = jnp.argsort(target_pos)  5.12 us
  transfers between devices with their start and end apart: 15, of which 7 were waited for; matrix products, arithmetic and copies ran while one was open for 15% of the time, Pallas kernels for 0%

commit v1 on v0

--- a/solution.py
+++ b/solution.py
@@ -5,6 +5,28 @@
 
 MOST = 4096
 FILL = -4.0
+
+
+def in_blocks(shard, dim, size):
+    before, after = (shard.shape[:dim], shard.shape[dim + 1 :])
+    return jnp.moveaxis(shard.reshape(*before, size, -1, *after), dim, 0)
+
+
+def joined_along(tiles, dim):
+    tiles = jnp.moveaxis(tiles, 0, dim)
+    shape = tiles.shape
+    return tiles.reshape(*shape[:dim], shape[dim] * shape[dim + 1], *shape[dim + 2 :])
+
+
+def swapped_with_each(x, axis, split_dim, concat_dim):
+    size, position = (lax.axis_size(axis), lax.axis_index(axis))
+    blocks = in_blocks(x, split_dim, size)
+    gathered = [blocks[position]]
+    for hop in range(1, size):
+        sent = blocks[position ^ hop]
+        gathered.append(lax.ppermute(sent, axis, [(i, i ^ hop) for i in range(size)]))
+    blocks = jnp.stack(gathered)[position ^ jnp.arange(size)]
+    return joined_along(blocks, concat_dim)
 
 
 def from_behind(block, axis, distance):
@@ -76,9 +98,7 @@
     returned_home = from_behind(visit_best, ("blk", "split"), -reach)
     best = jnp.maximum(best, returned_home)
     back = best[local].reshape(count, piece)
-    returned = lax.all_to_all(
-        back, ("blk", "split"), split_axis=0, concat_axis=0, tiled=True
-    ).reshape(rows)
+    returned = swapped_with_each(back, ("blk", "split"), 0, 0).reshape(rows)
     return jnp.zeros((rows,), jnp.float32).at[order].set(returned)
 
 

time: 204 us -> 217 us (1.064)
  starting transfers between devices: 17.1 us -> 37.5 us
  blocking collectives: 9.41 us -> 0 us
    ppermute x0 -> x15, starting transfers between devices: none -> 20.5 us  [swapped_with_each(): lax.ppermute(sent, axis, [(i, i ^ hop) for i in range(size)])]
    all_to_all x1 -> x0, blocking collectives: 9.41 us -> none  [body(): lax.all_to_all(back, ('blk', 'split'), split_axis=0, concat_axis=0, tiled...]
    ppermute x0 -> x15, waiting for transfers between devices: none -> 2.56 us  [swapped_with_each(): lax.ppermute(sent, axis, [(i, i ^ hop) for i in range(size)])]
  transfers between devices with their start and end apart: 15 -> 30, of which waited for: 7 -> 9; matrix products, arithmetic and copies ran while one was open for 15% -> 14% of each run, Pallas kernels for 0% -> 0%
where the time goes in v1:
time: 217 us
  waiting for transfers between devices  117 us (54%)
  local copies, waits for them, and re-layouts  40.9 us (19%)
  starting transfers between devices  37.5 us (17%)
  other arithmetic  11.7 us (5%)
  matrix products  9.56 us (4%)
    ppermute x13, waiting for transfers between devices, from_behind(): return lax.ppermute(block, axis, route)  93.9 us
    ppermute x15, starting transfers between devices, swapped_with_each(): lax.ppermute(sent, axis, [(i, i ^ hop) for i in range(size)])  20.5 us
    all_to_all x1, waiting for transfers between devices, body(): lax.all_to_all(packed, ('blk', 'split'), split_axis=0, concat_axis=0, til...  20.1 us
    dot_general x5, matrix products, masked_scores(): lax.dot_general(left, right, (((1,), (1,)), ((), ())), preferred_element_...  9.56 us
    all_to_all x1, starting transfers between devices, body(): lax.all_to_all(labels, ('blk', 'split'), split_axis=0, concat_axis=0, til...  7.41 us
    all_to_all x1, starting transfers between devices, body(): lax.all_to_all(packed, ('blk', 'split'), split_axis=0, concat_axis=0, til...  5.53 us
    gather x1, local copies, waits for them, and re-layouts, body(): packed = unit[order].reshape(count, piece, width)  5.21 us
    sort x1, other arithmetic, body(): order = jnp.argsort(target_pos)  5.12 us
  transfers between devices with their start and end apart: 30, of which 9 were waited for; matrix products, arithmetic and copies ran while one was open for 14% of the time, Pallas kernels for 0%

profile of v1, /device:TPU:0, one launch (start us, length us, event | category | flops | bytes accessed | tf_op | source)
XLA Modules:
  0.0 217.2 jit_solution(9462251945800347801)
XLA Ops:
  0.0 5.1 %sort.31 = (s32[1024]{0:T(1024)}, s32[1024]{0:T(1024)S(1)}) sort(s32[1024]{0:T(1024)} %param.7, s32[1024]{0:T(1024)S(1)} %iota.19), dimensions={0}, to_apply=%region_0.0 | sort | flops 10240 | bytes 16384 | tf_op jit(solution)/shard_map/jit(argsort)/sort | solution.py:54
  5.1 4.5 %gather_fusion.1 = s32[1024]{0:T(1024)S(1)} fusion(s32[1024]{0:T(1024)S(1)} %copy-done.1, s32[1024]{0:T(1024)S(1)} %get-tuple-element.108), kind=kCustom, calls=%fused_computation.1 | custom fusion | bytes 12288 | tf_op jit(solution)/shard_map/gather | solution.py:57
  9.7 0.1 stack_reshape.7
  9.8 4.5 %gather_fusion = s32[1024]{0:T(1024)S(1)} fusion(s32[1024]{0:T(1024)S(1)} %copy-done, s32[1024]{0:T(1024)S(1)} %get-tuple-element.108), kind=kCustom, calls=%fused_computation | custom fusion | bytes 12288 | tf_op jit(solution)/shard_map/gather | solution.py:57
  14.3 0.1 stack_reshape.6
  14.4 0.7 reshape.149
  15.1 7.4 %all-to-all-start = ((s32[16,1,128]{2,1,0:T(1,128)}), s32[16,1,128]{2,1,0:T(1,128)S(1)}, u32[]{:S(2)}, u32[]{:S(2)}) async-start(s32[16,1,128]{2,1,0:T(1,128)} %reshape.149), calls=%async_computation | async-start | bytes 16384 | tf_op jit(solution)/shard_map/all_to_all | solution.py:61
  22.5 0.4 fusion.2
  22.9 0.3 fusion.3
  23.2 5.2 %gather_fusion.3 = bf16[1024,768]{1,0:T(8,128)(2,1)} fusion(bf16[1024,768]{1,0:T(8,128)(2,1)S(1)} %fusion.3, s32[1024]{0:T(1024)S(1)} %get-tuple-element.108), kind=kCustom, calls=%fused_computation.3 | custom fusion | bytes 3149824 | tf_op jit(solution)/shard_map/gather | solution.py:55
  28.4 0.5 all-to-all-done
  28.9 5.5 %all-to-all-start.1 = ((bf16[16,64,768]{2,1,0:T(8,128)(2,1)}), bf16[16,64,768]{2,1,0:T(8,128)(2,1)S(1)}, u32[]{:S(2)}, u32[]{:S(2)}) async-start(bf16[16,64,768]{2,1,0:T(8,128)(2,1)} %bitcast), calls=%async_computation.1 | async-start | bytes 3145728 | tf_op jit(solution)/shard_map/all_to_all | solution.py:60
  34.6 0.5 broadcast.126
  35.1 0.7 reduce.11
  35.8 0.1 reshape.150
  35.8 0.5 broadcast.125
  36.4 0.7 fusion.23
  37.1 0.1 reshape_squeeze.4
  37.1 0.1 sub.21
  37.2 4.4 %sort.32 = (s32[1024]{0:T(1024)}, s32[1024]{0:T(1024)S(1)}) sort(s32[1024]{0:T(1024)S(1)} %sub.21, s32[1024]{0:T(1024)S(1)} %iota.20), dimensions={0}, to_apply=%region_1.0 | sort | flops 10240 | bytes 16384 | tf_op jit(solution)/shard_map/jit(argsort)/sort | solution.py:66
  41.6 4.5 %gather_fusion.2 = s32[1024]{0:T(1024)S(1)} fusion(s32[1024]{0:T(1024)S(1)} %reshape_squeeze.4, s32[1024]{0:T(1024)S(1)} %fusion.4), kind=kCustom, calls=%fused_computation.2 | custom fusion | bytes 12288 | tf_op jit(solution)/shard_map/gather | solution.py:68
  46.1 0.1 sub.22
  46.2 20.1 %all-to-all-done.1 = bf16[16,64,768]{2,1,0:T(8,128)(2,1)S(1)} async-done(((bf16[16,64,768]{2,1,0:T(8,128)(2,1)}), bf16[16,64,768]{2,1,0:T(8,128)(2,1)S(1)}, u32[]{:S(2)}, u32[]{:S(2)}) %all-to-all-start.1) | async-done | bytes 1572896 | tf_op jit(solution)/shard_map/all_to_all | solution.py:60
  66.3 4.0 %gather_fusion.4 = bf16[1024,768]{1,0:T(8,128)(2,1)S(1)} fusion(bf16[1024,768]{1,0:T(8,128)(2,1)S(1)} %bitcast.90, s32[1024]{0:T(1024)S(1)} %fusion.4), kind=kCustom, calls=%fused_computation.4 | custom fusion | bytes 3149824 | tf_op jit(solution)/shard_map/gather | solution.py:67
  70.3 1.8 select_reduce_fusion
  72.1 1.2 copy.36
  73.3 107.0 %while.17 = (s32[]{:T(128)}, f32[1024]{0:T(1024)S(1)}, bf16[1024,768]{1,0:T(8,128)(2,1)}, s32[1024]{0:T(1024)S(1)}, f32[1024]{0:T(1024)S(1)}, /*index=5*/s32[102...) while((s32[]{:T(128)}, f32[1024]{0:T(1024)S(1)}, bf16[1024,768]{1,0:T(8,128)(2,1)}, ...), condition=%wide.region_7.8_spmd.clone, body=%wide.region_4.0_spmd.clone.sunk | while | flops 1614809088 | bytes 12660959 | solution.py:95
  73.3 1.0 collective-permute-start.1
  74.3 1.8 collective-permute-start
  76.1 1.0 collective-permute-start.2
  77.1 22.3 %collective-permute-done = s32[1024]{0:T(1024)S(1)} collective-permute-done((s32[1024]{0:T(1024)S(1)}, s32[1024]{0:T(1024)S(1)}, u32[]{:S(2)}, u32[]{:S(2)}) %collective-permute-start) | collective-permute-done | bytes 4128 | tf_op jit(solution)/shard_map/while/body/eval_jaxpr/ppermute | solution.py:35
  99.4 1.9 fusion.33
  101.3 1.2 copy.46
  102.5 0.1 collective-permute-start
  102.7 22.6 %collective-permute-done = s32[1024]{0:T(1024)S(1)} collective-permute-done((s32[1024]{0:T(1024)S(1)}, s32[1024]{0:T(1024)S(1)}, u32[]{:S(2)}, u32[]{:S(2)}) %collective-permute-start) | collective-permute-done | bytes 4128 | tf_op jit(solution)/shard_map/while/body/eval_jaxpr/ppermute | solution.py:35
  125.3 1.9 fusion.33
  127.2 1.2 copy.46
  128.6 22.6 %collective-permute-done = s32[1024]{0:T(1024)S(1)} collective-permute-done((s32[1024]{0:T(1024)S(1)}, s32[1024]{0:T(1024)S(1)}, u32[]{:S(2)}, u32[]{:S(2)}) %collective-permute-start) | collective-permute-done | bytes 4128 | tf_op jit(solution)/shard_map/while/body/eval_jaxpr/ppermute | solution.py:35
  151.2 1.9 fusion.33
  153.1 1.2 copy.46
  154.5 22.7 %collective-permute-done = s32[1024]{0:T(1024)S(1)} collective-permute-done((s32[1024]{0:T(1024)S(1)}, s32[1024]{0:T(1024)S(1)}, u32[]{:S(2)}, u32[]{:S(2)}) %collective-permute-start) | collective-permute-done | bytes 4128 | tf_op jit(solution)/shard_map/while/body/eval_jaxpr/ppermute | solution.py:35
  177.2 1.9 fusion.33
  179.2 1.2 copy.46
  180.3 3.6 %collective-permute-done.3 = f32[1024]{0:T(1024)S(1)} collective-permute-done((f32[1024]{0:T(1024)S(1)}, f32[1024]{0:T(1024)S(1)}, u32[]{:S(2)}, u32[]{:S(2)}) %collective-permute-start.3) | collective-permute-done | bytes 4128 | tf_op jit(solution)/shard_map/ppermute | solution.py:35
  183.9 4.5 %gather_fusion.5 = f32[1024]{0:T(1024)S(1)} fusion(f32[1024]{0:T(1024)S(1)} %max.9, s32[1024]{0:T(1024)S(1)} %broadcast_clamp_fusion), kind=kCustom, calls=%fused_computation.5 | custom fusion | bytes 12288 | tf_op jit(solution)/shard_map/gather | solution.py:100
  188.5 0.1 reshape_reshape.6
  188.6 0.1 collective-permute-start.4
  188.7 0.1 collective-permute-start.5
  188.7 1.8 collective-permute-start.6
  190.5 1.7 collective-permute-start.8
  192.3 2.6 %collective-permute-start.10 = (f32[1,64]{1,0:T(1,128)S(1)}, f32[1,64]{1,0:T(1,128)S(1)}, u32[]{:S(2)}, u32[]{:S(2)}) collective-permute-start(f32[1,64]{1,0:T(1,128)S(1)} %get-tuple-element.100), channel_id=1, source_target_pairs={{0,7},{1,6},{2,5},{3,4},{4,3},{5,2},{6,1},{7,0},{8,15},{9,14},{10,... | collective-permute-start | bytes 776 | tf_op jit(solution)/shard_map/ppermute | solution.py:27
  194.9 0.3 collective-permute-start.11
  195.2 2.3 %collective-permute-start.12 = (f32[1,64]{1,0:T(1,128)S(1)}, f32[1,64]{1,0:T(1,128)S(1)}, u32[]{:S(2)}, u32[]{:S(2)}) collective-permute-start(f32[1,64]{1,0:T(1,128)S(1)} %get-tuple-element.98), channel_id=1, source_target_pairs={{0,9},{1,8},{2,11},{3,10},{4,13},{5,12},{6,15},{7,14},{8,1},{9,0},... | collective-permute-start | bytes 776 | tf_op jit(solution)/shard_map/ppermute | solution.py:27
  197.5 0.4 collective-permute-start.13
  198.0 3.1 %collective-permute-start.14 = (f32[1,64]{1,0:T(1,128)S(1)}, f32[1,64]{1,0:T(1,128)S(1)}, u32[]{:S(2)}, u32[]{:S(2)}) collective-permute-start(f32[1,64]{1,0:T(1,128)S(1)} %get-tuple-element.96), channel_id=1, source_target_pairs={{0,11},{1,10},{2,9},{3,8},{4,15},{5,14},{6,13},{7,12},{8,3},{9,2},... | collective-permute-start | bytes 776 | tf_op jit(solution)/shard_map/ppermute | solution.py:27
  201.1 1.8 collective-permute-start.15
  202.9 1.7 collective-permute-start.16
  204.6 1.3 collective-permute-start.17
  205.9 3.2 %collective-permute-start.18 = (f32[1,64]{1,0:T(1,128)S(1)}, f32[1,64]{1,0:T(1,128)S(1)}, u32[]{:S(2)}, u32[]{:S(2)}) collective-permute-start(f32[1,64]{1,0:T(1,128)S(1)} %get-tuple-element.92), channel_id=1, source_target_pairs={{0,15},{1,14},{2,13},{3,12},{4,11},{5,10},{6,9},{7,8},{8,7},{9,6},... | collective-permute-start | bytes 776 | tf_op jit(solution)/shard_map/ppermute | solution.py:27
  209.1 1.7 collective-permute-done.17
  210.9 0.7 collective-permute-done.18
  211.7 0.6 gather_fusion.6
  212.2 0.1 reshape.119
  212.3 4.9 %scatter_custom_fusion = f32[1024]{0:T(1024)} fusion(s32[1024]{0:T(1024)S(1)} %get-tuple-element.109, f32[1024]{0:T(1024)S(1)} %reshape.119, f32[]{:T(128)} %constant.32.clone.1), kind=kCustom, calls=%fused_computation.47 | custom fusion | bytes 4100 | tf_op jit(solution)/shard_map/scatter | solution.py:102
  (69 shorter events, 0.7 us)
Async XLA Ops:
  0.0 9.8 %copy-start = (s32[1024]{0:T(1024)S(1)}, s32[1024]{0:T(1024)}, u32[]{:S(2)}) copy-start(s32[1024]{0:T(1024)} %param.6) | copy-start | bytes 12292
  0.0 5.1 %copy-start.1 = (s32[1024]{0:T(1024)S(1)}, s32[1024]{0:T(1024)}, u32[]{:S(2)}) copy-start(s32[1024]{0:T(1024)} %param.7) | copy-start | bytes 12292
  9.8 12.7 %copy-start.2 = (bf16[1024,768]{1,0:T(8,128)(2,1)S(1)}, bf16[1024,768]{1,0:T(8,128)(2,1)}, u32[]{:S(2)}) copy-start(bf16[1024,768]{1,0:T(8,128)(2,1)} %param.5) | copy-start | bytes 4718596
  15.1 13.8 %all-to-all-start = ((s32[16,1,128]{2,1,0:T(1,128)}), s32[16,1,128]{2,1,0:T(1,128)S(1)}, u32[]{:S(2)}, u32[]{:S(2)}) async-start(s32[16,1,128]{2,1,0:T(1,128)} %reshape.149), calls=%async_computation | async-start | bytes 16384 | tf_op jit(solution)/shard_map/all_to_all | solution.py:61
  28.9 37.4 %all-to-all-start.1 = ((bf16[16,64,768]{2,1,0:T(8,128)(2,1)}), bf16[16,64,768]{2,1,0:T(8,128)(2,1)S(1)}, u32[]{:S(2)}, u32[]{:S(2)}) async-start(bf16[16,64,768]{2,1,0:T(8,128)(2,1)} %bitcast), calls=%async_computation.1 | async-start | bytes 3145728 | tf_op jit(solution)/shard_map/all_to_all | solution.py:60
  73.3 26.1 %collective-permute-start.1 = (bf16[1024,768]{1,0:T(8,128)(2,1)}, bf16[1024,768]{1,0:T(8,128)(2,1)S(1)}, u32[]{:S(2)}, u32[]{:S(2)}) collective-permute-start(bf16[1024,768]{1,0:T(8,128)(2,1)} %get-tuple-element.168), channel_id=1, source_target_pairs={{15,0},{0,1},{1,2},{2,3},{3,4},{4,5},{5,6},{6,7},{7,8},{8,9},{9,10... | collective-permute-start | bytes 4718600 | tf_op jit(solution)/shard_map/while/body/eval_jaxpr/ppermute | solution.py:35
  74.3 25.1 %collective-permute-start = (s32[1024]{0:T(1024)S(1)}, s32[1024]{0:T(1024)S(1)}, u32[]{:S(2)}, u32[]{:S(2)}) collective-permute-start(s32[1024]{0:T(1024)S(1)} %get-tuple-element.169), channel_id=1, source_target_pairs={{15,0},{0,1},{1,2},{2,3},{3,4},{4,5},{5,6},{6,7},{7,8},{8,9},{9,10... | collective-permute-start | bytes 12296 | tf_op jit(solution)/shard_map/while/body/eval_jaxpr/ppermute | solution.py:35
  76.1 26.4 %collective-permute-start.2 = (bf16[1024]{0:T(1024)(128)(2,1)S(1)}, bf16[1024]{0:T(1024)(128)(2,1)S(1)}, u32[]{:S(2)}, u32[]{:S(2)}) collective-permute-start(bf16[1024]{0:T(1024)(128)(2,1)S(1)} %select_convert_fusion.2), channel_id=1, source_target_pairs={{15,0},{0,1},{1,2},{2,3},{3,4},{4,5},{5,6},{6,7},{7,8},{8,9},{9,10... | collective-permute-start | bytes 6152 | tf_op jit(solution)/shard_map/while/body/eval_jaxpr/ppermute | solution.py:35
  102.5 22.8 %collective-permute-start.1 = (bf16[1024,768]{1,0:T(8,128)(2,1)}, bf16[1024,768]{1,0:T(8,128)(2,1)S(1)}, u32[]{:S(2)}, u32[]{:S(2)}) collective-permute-start(bf16[1024,768]{1,0:T(8,128)(2,1)} %get-tuple-element.168), channel_id=1, source_target_pairs={{15,0},{0,1},{1,2},{2,3},{3,4},{4,5},{5,6},{6,7},{7,8},{8,9},{9,10... | collective-permute-start | bytes 4718600 | tf_op jit(solution)/shard_map/while/body/eval_jaxpr/ppermute | solution.py:35
  102.5 22.8 %collective-permute-start = (s32[1024]{0:T(1024)S(1)}, s32[1024]{0:T(1024)S(1)}, u32[]{:S(2)}, u32[]{:S(2)}) collective-permute-start(s32[1024]{0:T(1024)S(1)} %get-tuple-element.169), channel_id=1, source_target_pairs={{15,0},{0,1},{1,2},{2,3},{3,4},{4,5},{5,6},{6,7},{7,8},{8,9},{9,10... | collective-permute-start | bytes 12296 | tf_op jit(solution)/shard_map/while/body/eval_jaxpr/ppermute | solution.py:35
  102.6 25.8 %collective-permute-start.2 = (bf16[1024]{0:T(1024)(128)(2,1)S(1)}, bf16[1024]{0:T(1024)(128)(2,1)S(1)}, u32[]{:S(2)}, u32[]{:S(2)}) collective-permute-start(bf16[1024]{0:T(1024)(128)(2,1)S(1)} %select_convert_fusion.2), channel_id=1, source_target_pairs={{15,0},{0,1},{1,2},{2,3},{3,4},{4,5},{5,6},{6,7},{7,8},{8,9},{9,10... | collective-permute-start | bytes 6152 | tf_op jit(solution)/shard_map/while/body/eval_jaxpr/ppermute | solution.py:35
  128.4 22.8 %collective-permute-start.1 = (bf16[1024,768]{1,0:T(8,128)(2,1)}, bf16[1024,768]{1,0:T(8,128)(2,1)S(1)}, u32[]{:S(2)}, u32[]{:S(2)}) collective-permute-start(bf16[1024,768]{1,0:T(8,128)(2,1)} %get-tuple-element.168), channel_id=1, source_target_pairs={{15,0},{0,1},{1,2},{2,3},{3,4},{4,5},{5,6},{6,7},{7,8},{8,9},{9,10... | collective-permute-start | bytes 4718600 | tf_op jit(solution)/shard_map/while/body/eval_jaxpr/ppermute | solution.py:35
  128.4 22.8 %collective-permute-start = (s32[1024]{0:T(1024)S(1)}, s32[1024]{0:T(1024)S(1)}, u32[]{:S(2)}, u32[]{:S(2)}) collective-permute-start(s32[1024]{0:T(1024)S(1)} %get-tuple-element.169), channel_id=1, source_target_pairs={{15,0},{0,1},{1,2},{2,3},{3,4},{4,5},{5,6},{6,7},{7,8},{8,9},{9,10... | collective-permute-start | bytes 12296 | tf_op jit(solution)/shard_map/while/body/eval_jaxpr/ppermute | solution.py:35
  128.5 25.8 %collective-permute-start.2 = (bf16[1024]{0:T(1024)(128)(2,1)S(1)}, bf16[1024]{0:T(1024)(128)(2,1)S(1)}, u32[]{:S(2)}, u32[]{:S(2)}) collective-permute-start(bf16[1024]{0:T(1024)(128)(2,1)S(1)} %select_convert_fusion.2), channel_id=1, source_target_pairs={{15,0},{0,1},{1,2},{2,3},{3,4},{4,5},{5,6},{6,7},{7,8},{8,9},{9,10... | collective-permute-start | bytes 6152 | tf_op jit(solution)/shard_map/while/body/eval_jaxpr/ppermute | solution.py:35
  154.3 22.9 %collective-permute-start.1 = (bf16[1024,768]{1,0:T(8,128)(2,1)}, bf16[1024,768]{1,0:T(8,128)(2,1)S(1)}, u32[]{:S(2)}, u32[]{:S(2)}) collective-permute-start(bf16[1024,768]{1,0:T(8,128)(2,1)} %get-tuple-element.168), channel_id=1, source_target_pairs={{15,0},{0,1},{1,2},{2,3},{3,4},{4,5},{5,6},{6,7},{7,8},{8,9},{9,10... | collective-permute-start | bytes 4718600 | tf_op jit(solution)/shard_map/while/body/eval_jaxpr/ppermute | solution.py:35
  154.3 22.9 %collective-permute-start = (s32[1024]{0:T(1024)S(1)}, s32[1024]{0:T(1024)S(1)}, u32[]{:S(2)}, u32[]{:S(2)}) collective-permute-start(s32[1024]{0:T(1024)S(1)} %get-tuple-element.169), channel_id=1, source_target_pairs={{15,0},{0,1},{1,2},{2,3},{3,4},{4,5},{5,6},{6,7},{7,8},{8,9},{9,10... | collective-permute-start | bytes 12296 | tf_op jit(solution)/shard_map/while/body/eval_jaxpr/ppermute | solution.py:35
  154.4 25.9 %collective-permute-start.2 = (bf16[1024]{0:T(1024)(128)(2,1)S(1)}, bf16[1024]{0:T(1024)(128)(2,1)S(1)}, u32[]{:S(2)}, u32[]{:S(2)}) collective-permute-start(bf16[1024]{0:T(1024)(128)(2,1)S(1)} %select_convert_fusion.2), channel_id=1, source_target_pairs={{15,0},{0,1},{1,2},{2,3},{3,4},{4,5},{5,6},{6,7},{7,8},{8,9},{9,10... | collective-permute-start | bytes 6152 | tf_op jit(solution)/shard_map/while/body/eval_jaxpr/ppermute | solution.py:35
  180.3 3.6 %collective-permute-start.3 = (f32[1024]{0:T(1024)S(1)}, f32[1024]{0:T(1024)S(1)}, u32[]{:S(2)}, u32[]{:S(2)}) collective-permute-start(f32[1024]{0:T(1024)S(1)} %get-tuple-element.48), channel_id=1, source_target_pairs={{4,0},{5,1},{6,2},{7,3},{8,4},{9,5},{10,6},{11,7},{12,8},{13,9},{1... | collective-permute-start | bytes 12296 | tf_op jit(solution)/shard_map/ppermute | solution.py:35
  188.6 3.6 %collective-permute-start.4 = (f32[1,64]{1,0:T(1,128)S(1)}, f32[1,64]{1,0:T(1,128)S(1)}, u32[]{:S(2)}, u32[]{:S(2)}) collective-permute-start(f32[1,64]{1,0:T(1,128)S(1)} %get-tuple-element.106), channel_id=1, source_target_pairs={{0,1},{1,0},{2,3},{3,2},{4,5},{5,4},{6,7},{7,6},{8,9},{9,8},{10,11... | collective-permute-start | bytes 776 | tf_op jit(solution)/shard_map/ppermute | solution.py:27
  188.7 3.6 %collective-permute-start.5 = (f32[1,64]{1,0:T(1,128)S(1)}, f32[1,64]{1,0:T(1,128)S(1)}, u32[]{:S(2)}, u32[]{:S(2)}) collective-permute-start(f32[1,64]{1,0:T(1,128)S(1)} %get-tuple-element.105), channel_id=1, source_target_pairs={{0,2},{1,3},{2,0},{3,1},{4,6},{5,7},{6,4},{7,5},{8,10},{9,11},{10,... | collective-permute-start | bytes 776 | tf_op jit(solution)/shard_map/ppermute | solution.py:27
  188.7 6.2 %collective-permute-start.6 = (f32[1,64]{1,0:T(1,128)S(1)}, f32[1,64]{1,0:T(1,128)S(1)}, u32[]{:S(2)}, u32[]{:S(2)}) collective-permute-start(f32[1,64]{1,0:T(1,128)S(1)} %get-tuple-element.104), channel_id=1, source_target_pairs={{0,3},{1,2},{2,1},{3,0},{4,7},{5,6},{6,5},{7,4},{8,11},{9,10},{10,... | collective-permute-start | bytes 776 | tf_op jit(solution)/shard_map/ppermute | solution.py:27
  190.5 4.7 %collective-permute-start.7 = (f32[1,64]{1,0:T(1,128)S(1)}, f32[1,64]{1,0:T(1,128)S(1)}, u32[]{:S(2)}, u32[]{:S(2)}) collective-permute-start(f32[1,64]{1,0:T(1,128)S(1)} %get-tuple-element.103), channel_id=1, source_target_pairs={{0,4},{1,5},{2,6},{3,7},{4,0},{5,1},{6,2},{7,3},{8,12},{9,13},{10,... | collective-permute-start | bytes 776 | tf_op jit(solution)/shard_map/ppermute | solution.py:27
  190.5 7.0 %collective-permute-start.8 = (f32[1,64]{1,0:T(1,128)S(1)}, f32[1,64]{1,0:T(1,128)S(1)}, u32[]{:S(2)}, u32[]{:S(2)}) collective-permute-start(f32[1,64]{1,0:T(1,128)S(1)} %get-tuple-element.102), channel_id=1, source_target_pairs={{0,5},{1,4},{2,7},{3,6},{4,1},{5,0},{6,3},{7,2},{8,13},{9,12},{10,... | collective-permute-start | bytes 776 | tf_op jit(solution)/shard_map/ppermute | solution.py:27
  192.2 5.8 %collective-permute-start.9 = (f32[1,64]{1,0:T(1,128)S(1)}, f32[1,64]{1,0:T(1,128)S(1)}, u32[]{:S(2)}, u32[]{:S(2)}) collective-permute-start(f32[1,64]{1,0:T(1,128)S(1)} %get-tuple-element.101), channel_id=1, source_target_pairs={{0,6},{1,7},{2,4},{3,5},{4,2},{5,3},{6,0},{7,1},{8,14},{9,15},{10,... | collective-permute-start | bytes 776 | tf_op jit(solution)/shard_map/ppermute | solution.py:27
  192.3 8.8 %collective-permute-start.10 = (f32[1,64]{1,0:T(1,128)S(1)}, f32[1,64]{1,0:T(1,128)S(1)}, u32[]{:S(2)}, u32[]{:S(2)}) collective-permute-start(f32[1,64]{1,0:T(1,128)S(1)} %get-tuple-element.100), channel_id=1, source_target_pairs={{0,7},{1,6},{2,5},{3,4},{4,3},{5,2},{6,1},{7,0},{8,15},{9,14},{10,... | collective-permute-start | bytes 776 | tf_op jit(solution)/shard_map/ppermute | solution.py:27
  194.9 8.0 %collective-permute-start.11 = (f32[1,64]{1,0:T(1,128)S(1)}, f32[1,64]{1,0:T(1,128)S(1)}, u32[]{:S(2)}, u32[]{:S(2)}) collective-permute-start(f32[1,64]{1,0:T(1,128)S(1)} %get-tuple-element.99), channel_id=1, source_target_pairs={{0,8},{1,9},{2,10},{3,11},{4,12},{5,13},{6,14},{7,15},{8,0},{9,1},... | collective-permute-start | bytes 776 | tf_op jit(solution)/shard_map/ppermute | solution.py:27
  195.2 9.4 %collective-permute-start.12 = (f32[1,64]{1,0:T(1,128)S(1)}, f32[1,64]{1,0:T(1,128)S(1)}, u32[]{:S(2)}, u32[]{:S(2)}) collective-permute-start(f32[1,64]{1,0:T(1,128)S(1)} %get-tuple-element.98), channel_id=1, source_target_pairs={{0,9},{1,8},{2,11},{3,10},{4,13},{5,12},{6,15},{7,14},{8,1},{9,0},... | collective-permute-start | bytes 776 | tf_op jit(solution)/shard_map/ppermute | solution.py:27
  197.5 8.4 %collective-permute-start.13 = (f32[1,64]{1,0:T(1,128)S(1)}, f32[1,64]{1,0:T(1,128)S(1)}, u32[]{:S(2)}, u32[]{:S(2)}) collective-permute-start(f32[1,64]{1,0:T(1,128)S(1)} %get-tuple-element.97), channel_id=1, source_target_pairs={{0,10},{1,11},{2,8},{3,9},{4,14},{5,15},{6,12},{7,13},{8,2},{9,3},... | collective-permute-start | bytes 776 | tf_op jit(solution)/shard_map/ppermute | solution.py:27
  198.0 11.1 %collective-permute-start.14 = (f32[1,64]{1,0:T(1,128)S(1)}, f32[1,64]{1,0:T(1,128)S(1)}, u32[]{:S(2)}, u32[]{:S(2)}) collective-permute-start(f32[1,64]{1,0:T(1,128)S(1)} %get-tuple-element.96), channel_id=1, source_target_pairs={{0,11},{1,10},{2,9},{3,8},{4,15},{5,14},{6,13},{7,12},{8,3},{9,2},... | collective-permute-start | bytes 776 | tf_op jit(solution)/shard_map/ppermute | solution.py:27
  201.1 8.0 %collective-permute-start.15 = (f32[1,64]{1,0:T(1,128)S(1)}, f32[1,64]{1,0:T(1,128)S(1)}, u32[]{:S(2)}, u32[]{:S(2)}) collective-permute-start(f32[1,64]{1,0:T(1,128)S(1)} %get-tuple-element.95), channel_id=1, source_target_pairs={{0,12},{1,13},{2,14},{3,15},{4,8},{5,9},{6,10},{7,11},{8,4},{9,5},... | collective-permute-start | bytes 776 | tf_op jit(solution)/shard_map/ppermute | solution.py:27
  202.9 6.2 %collective-permute-start.16 = (f32[1,64]{1,0:T(1,128)S(1)}, f32[1,64]{1,0:T(1,128)S(1)}, u32[]{:S(2)}, u32[]{:S(2)}) collective-permute-start(f32[1,64]{1,0:T(1,128)S(1)} %get-tuple-element.94), channel_id=1, source_target_pairs={{0,13},{1,12},{2,15},{3,14},{4,9},{5,8},{6,11},{7,10},{8,5},{9,4},... | collective-permute-start | bytes 776 | tf_op jit(solution)/shard_map/ppermute | solution.py:27
  204.6 6.3 %collective-permute-start.17 = (f32[1,64]{1,0:T(1,128)S(1)}, f32[1,64]{1,0:T(1,128)S(1)}, u32[]{:S(2)}, u32[]{:S(2)}) collective-permute-start(f32[1,64]{1,0:T(1,128)S(1)} %get-tuple-element.93), channel_id=1, source_target_pairs={{0,14},{1,15},{2,12},{3,13},{4,10},{5,11},{6,8},{7,9},{8,6},{9,7},... | collective-permute-start | bytes 776 | tf_op jit(solution)/shard_map/ppermute | solution.py:27
  205.9 5.7 %collective-permute-start.18 = (f32[1,64]{1,0:T(1,128)S(1)}, f32[1,64]{1,0:T(1,128)S(1)}, u32[]{:S(2)}, u32[]{:S(2)}) collective-permute-start(f32[1,64]{1,0:T(1,128)S(1)} %get-tuple-element.92), channel_id=1, source_target_pairs={{0,15},{1,14},{2,13},{3,12},{4,11},{5,10},{6,9},{7,8},{8,7},{9,6},... | collective-permute-start | bytes 776 | tf_op jit(solution)/shard_map/ppermute | solution.py:27
